TPU v7x, 32 devices: a whole 2x2x4 slice. The times are simulated.
32 devices in a mesh: dp: 8 (over z, y), tensor: 4 (over x, core).
Axes of the slice: x: 2, y: 2, z: 4, core: 2. Of those that a mesh axis runs over, the one named last changes fastest.
Arguments:
- tokens: bfloat16 [2048, 1024], P('dp'), may hold values from -6 to 6
- norm_first: float32 [1024], replicated, may hold values from 0.25 to 1.75
- w_in: bfloat16 [1024, 3, 1024], P(None, None, 'tensor'), may hold values from -0.1875 to 0.1875
- conv_taps: float32 [3, 1024], P(None, 'tensor'), may hold values from -1 to 1
- w_out: bfloat16 [1024, 1024], P('tensor'), may hold values from -0.1875 to 0.1875
- norm_second: float32 [1024], replicated, may hold values from 0.25 to 1.75
- w_gate_up: bfloat16 [1024, 2, 4608], P(None, None, 'tensor'), may hold values from -0.1875 to 0.1875
- w_down: bfloat16 [4608, 1024], P('tensor'), may hold values from -0.09375 to 0.09375
- cotangent: bfloat16 [2048, 1024], P('dp'), may hold values from -6 to 6
Outputs:
- block_out: bfloat16 [2048, 1024], P('dp')
- grad_tokens: float32 [2048, 1024], P('dp')
- grad_norm_first: float32 [1024], replicated
- grad_w_in: float32 [1024, 3, 1024], P('dp', None, 'tensor')
- grad_taps: float32 [3, 1024], P(None, 'tensor')
- grad_w_out: float32 [1024, 1024], P('tensor', 'dp')
- grad_norm_second: float32 [1024], replicated
- grad_w_gate_up: float32 [1024, 2, 4608], P('dp', None, 'tensor')
- grad_w_down: float32 [4608, 1024], P('tensor', 'dp')
All inputs are finite; a program needn't handle non-finite values.
Results may differ from a plain program's by a relative error of at most 0.011.
Values sent between devices are 32-bit elements; how exact they have to be, the bound alone decides.
No kernel may reach another device: no remote copies, remote signals or barrier semaphores. Data moves between devices by JAX's collectives and lax.ppermute only.
A program may use at most 128 MiB of HBM per device.

v0:
```python
import jax
import jax.numpy as jnp
from jax import lax
from jax.sharding import PartitionSpec as P

eps = 1e-05


def shift_down(values, count):
    pad = jnp.zeros((count, values.shape[1]), values.dtype)
    return jnp.concatenate([pad, values[: values.shape[0] - count]], axis=0)


def shift_up(values, count):
    pad = jnp.zeros((count, values.shape[1]), values.dtype)
    return jnp.concatenate([values[count:], pad], axis=0)


def cross(left, right):
    return lax.dot_general(
        left, right, (((0,), (0,)), ((), ())), preferred_element_type=jnp.float32
    )


def by_transpose(left, right):
    return lax.dot_general(
        left, right, (((1,), (1,)), ((), ())), preferred_element_type=jnp.float32
    )


def body(tokens, norm_first, w_in, conv_taps, w_out, norm_second, w_gate_up, w_down, cotangent):
    rows, width = tokens.shape
    chans = w_in.shape[2]
    hid = w_down.shape[0]
    w_in_flat = w_in.reshape(width, 3 * chans)
    w_gu_flat = w_gate_up.reshape(width, 2 * hid)
    xf = tokens.astype(jnp.float32)
    s1 = lax.rsqrt(jnp.mean(xf * xf, axis=-1, keepdims=True) + eps)
    normed1 = (xf * s1 * norm_first).astype(jnp.bfloat16)
    proj = jnp.dot(normed1, w_in_flat, preferred_element_type=jnp.float32).reshape(rows, 3, chans)
    gate_b, gate_c, value = (proj[:, 0], proj[:, 1], proj[:, 2])
    mixed_in = gate_b * value
    conv = (
        conv_taps[0] * shift_down(mixed_in, 2)
        + conv_taps[1] * shift_down(mixed_in, 1)
        + conv_taps[2] * mixed_in
    )
    gated = (gate_c * conv).astype(jnp.bfloat16)
    mix = lax.psum(jnp.dot(gated, w_out, preferred_element_type=jnp.float32), "tensor")
    resid = xf + mix
    s2 = lax.rsqrt(jnp.mean(resid * resid, axis=-1, keepdims=True) + eps)
    normed2 = (resid * s2 * norm_second).astype(jnp.bfloat16)
    gate_up = jnp.dot(normed2, w_gu_flat, preferred_element_type=jnp.float32).reshape(rows, 2, hid)
    act, up = (gate_up[:, 0], gate_up[:, 1])
    sig = jax.nn.sigmoid(act)
    hidden = (act * sig * up).astype(jnp.bfloat16)
    ffn = lax.psum(jnp.dot(hidden, w_down, preferred_element_type=jnp.float32), "tensor")
    block_out = (resid + ffn).astype(jnp.bfloat16)
    cotf = cotangent.astype(jnp.float32)
    grad_down = cross(hidden, cotangent)
    d_hidden = by_transpose(cotangent, w_down)
    d_act = d_hidden * up * sig * (1.0 + act * (1.0 - sig))
    d_up = d_hidden * act * sig
    d_gu = jnp.stack([d_act, d_up], axis=1).astype(jnp.bfloat16).reshape(rows, 2 * hid)
    grad_gu = cross(normed2, d_gu).reshape(width, 2, hid)
    d_normed2 = lax.psum(by_transpose(d_gu, w_gu_flat), "tensor")
    gn2 = jnp.sum(d_normed2 * resid * s2, axis=0)
    weighted2 = d_normed2 * norm_second
    d_resid = (
        cotf + s2 * weighted2 - resid * s2**3 * jnp.mean(weighted2 * resid, axis=-1, keepdims=True)
    )
    d_resid_b = d_resid.astype(jnp.bfloat16)
    grad_out = cross(gated, d_resid_b)
    d_gated = by_transpose(d_resid_b, w_out)
    d_c = d_gated * conv
    d_conv = d_gated * gate_c
    gtaps = jnp.stack(
        [
            jnp.sum(d_conv * shift_down(mixed_in, 2), axis=0),
            jnp.sum(d_conv * shift_down(mixed_in, 1), axis=0),
            jnp.sum(d_conv * mixed_in, axis=0),
        ],
        axis=0,
    )
    d_mixed = (
        conv_taps[2] * d_conv
        + conv_taps[1] * shift_up(d_conv, 1)
        + conv_taps[0] * shift_up(d_conv, 2)
    )
    d_proj = (
        jnp.stack([d_mixed * value, d_c, d_mixed * gate_b], axis=1)
        .astype(jnp.bfloat16)
        .reshape(rows, 3 * chans)
    )
    grad_in = cross(normed1, d_proj).reshape(width, 3, chans)
    d_normed1 = lax.psum(by_transpose(d_proj, w_in_flat), "tensor")
    gn1 = jnp.sum(d_normed1 * xf * s1, axis=0)
    weighted1 = d_normed1 * norm_first
    grad_tokens = (
        d_resid + s1 * weighted1 - xf * s1**3 * jnp.mean(weighted1 * xf, axis=-1, keepdims=True)
    )
    shared_in, shared_out, shared_gu, shared_down = (
        lax.psum_scatter(grad_in, "dp", scatter_dimension=0, tiled=True),
        lax.psum_scatter(grad_out, "dp", scatter_dimension=1, tiled=True),
        lax.psum_scatter(grad_gu, "dp", scatter_dimension=0, tiled=True),
        lax.psum_scatter(grad_down, "dp", scatter_dimension=1, tiled=True),
    )
    sum_taps, sum_n1, sum_n2 = lax.psum((gtaps, gn1, gn2), "dp")
    return (
        block_out,
        grad_tokens,
        sum_n1,
        shared_in,
        sum_taps,
        shared_out,
        sum_n2,
        shared_gu,
        shared_down,
    )


def solution(mesh):
    return jax.shard_map(
        body,
        mesh=mesh,
        in_specs=(
            P("dp", None),
            P(),
            P(None, None, "tensor"),
            P(None, "tensor"),
            P("tensor", None),
            P(),
            P(None, None, "tensor"),
            P("tensor", None),
            P("dp", None),
        ),
        out_specs=(
            P("dp", None),
            P("dp", None),
            P(),
            P("dp", None, "tensor"),
            P(None, "tensor"),
            P("tensor", "dp"),
            P(),
            P("dp", None, "tensor"),
            P("tensor", "dp"),
        ),
        check_vma=False,
    )
```

profile of v0, /device:TPU:0, one launch (start us, length us, event | category | flops | bytes accessed | tf_op | source)
XLA Modules:
  0.0 582.6 jit_solution(139281299403452561)
XLA Ops:
  7.2 1.4 fusion.9
  10.0 2.7 copy.24
  12.7 2.1 fusion.2
  16.3 1.3 fusion.34
  17.6 5.4 copy.37
  23.0 6.7 %copy.25 = bf16[2304,1024]{1,0:T(8,128)(2,1)} copy(bf16[2304,1024]{0,1:T(8,128)(2,1)} %bitcast.107) | data formatting | bytes 9437184 | tf_op jit(solution)/shard_map/dot_general | solution.py:53
  29.6 27.1 %all-reduce.10.cloned.1.call-done = f32[256,1024]{1,0:T(8,128)} async-done(((f32[256,1024]{1,0:T(8,128)}), f32[256,1024]{1,0:T(8,128)}) %all-reduce.10.cloned.1.call-update) | async-done | bytes 1048592 | tf_op jit(solution)/shard_map/psum | solution.py:49
  56.8 1.6 multiply_reduce_fusion.2
  58.9 3.9 fusion.30
  62.9 1.2 multiply_bitcast_fusion.1
  65.3 2.4 fusion.4
  67.8 2.0 multiply_convert_fusion
  70.6 1.9 fusion.35
  72.5 32.2 %all-reduce.12.cloned.1.call-done = f32[256,1024]{1,0:T(8,128)} async-done(((f32[256,1024]{1,0:T(8,128)}), f32[256,1024]{1,0:T(8,128)}) %all-reduce.12.cloned.1.call-update) | async-done | bytes 1048592 | tf_op jit(solution)/shard_map/psum | solution.py:66
  104.7 1.6 multiply_reduce_fusion
  107.7 1.1 multiply_reduce_fusion.5
  110.7 1.6 convolution_bitcast_fusion
  112.6 2.4 maximum_convert_fusion
  115.0 2.4 copy.29
  117.4 6.8 %fusion.7 = f32[1024,2,1152]{2,0,1:T(8,128)} fusion(bf16[256,2,1152]{0,2,1:T(8,128)(2,1)} %copy.29, f32[256,1024]{1,0:T(8,128)S(1)} %get-tuple-element.43, f32[1024]{0:T(1024)S(1)} %copy-done.21, f32[256]{0:T(256)S(1)} %get-tuple-element.54), kind=kOutput, calls=%fused_computation.15 | convolution fusion | flops 1208745984 | bytes 11670528 | tf_op jit(solution)/shard_map/dot_general | solution.py:20
  124.3 2.5 fusion.23
  126.9 3.5 fusion.19
  130.5 4.2 fusion.36
  135.5 28.9 %all-reduce.14.cloned.1.call-done = (f32[256,1024]{1,0:T(8,128)}, f32[256,1024]{1,0:T(8,128)}) async-done(((f32[256,1024]{1,0:T(8,128)}, f32[256,1024]{1,0:T(8,128)}), (f32[256,1024]{1,0:T(8,128)}, f32[256,1024]{1,0:T(8,128)})) %all-reduce.14.cloned.1.call-update) | async-done | bytes 2097168 | tf_op jit(solution)/shard_map/psum | solution.py:57
  164.4 1.7 fusion.16
  166.1 39.2 %all-reduce.4 = (f32[1024]{0:T(1024)}, f32[3,256]{1,0:T(4,128)}, f32[1024]{0:T(1024)}) all-reduce(f32[1024]{0:T(1024)S(1)} %get-tuple-element.29, f32[3,256]{1,0:T(4,128)S(1)} %pad_maximum_fusion, f32[1024]{0:T(1024)S(1)} %get-tuple-element.27), channel_id=1, replica_groups=mesh['dp'=8,'tensor'=4] {'dp'}, use_global_device_ids=true, to_apply=%region_9.0 | all-reduce | flops 2816 | bytes 22528 | tf_op jit(solution)/shard_map/psum | solution.py:108
  205.3 3.5 fusion.13
  208.7 121.8 %reduce-scatter.9.cloned.1.call-done = f32[128,2,1152]{2,0,1:T(8,128)} async-done(((f32[1024,2,1152]{2,0,1:T(8,128)}), f32[128,2,1152]{2,0,1:T(8,128)}) %reduce-scatter.9.cloned.1.call-update) | async-done | bytes 1179664 | tf_op jit(solution)/shard_map/reduce_scatter | solution.py:105
  330.6 3.2 copy.31
  333.8 64.5 %reduce-scatter.7.cloned.1.call-done = f32[256,128]{1,0:T(8,128)} async-done(((f32[256,1024]{1,0:T(8,128)}), f32[256,128]{1,0:T(8,128)}) %reduce-scatter.7.cloned.1.call-update) | async-done | bytes 131088 | tf_op jit(solution)/shard_map/reduce_scatter | solution.py:104
  398.3 77.9 %reduce-scatter.5.cloned.1.call-done = f32[128,3,256]{2,0,1:T(8,128)} async-done(((f32[1024,3,256]{2,0,1:T(8,128)}), f32[128,3,256]{2,0,1:T(8,128)}) %reduce-scatter.5.cloned.1.call-update) | async-done | bytes 393232 | tf_op jit(solution)/shard_map/reduce_scatter | solution.py:103
  476.2 99.5 %reduce-scatter.11.cloned.1.call-done = f32[1152,128]{1,0:T(8,128)} async-done(((f32[1152,1024]{1,0:T(8,128)}), f32[1152,128]{1,0:T(8,128)}) %reduce-scatter.11.cloned.1.call-update) | async-done | bytes 589840 | tf_op jit(solution)/shard_map/reduce_scatter | solution.py:106
  (105 shorter events, 10.0 us)
Async XLA Ops:
  7.2 55.7 %copy-start = (bf16[1152,1024]{1,0:T(8,128)(2,1)S(1)}, bf16[1152,1024]{1,0:T(8,128)(2,1)}, u32[]{:S(2)}) copy-start(bf16[1152,1024]{1,0:T(8,128)(2,1)} %param.16) | copy-start | bytes 7077892
  7.2 49.6 %all-reduce.10.cloned.1.call-start = ((), (), s32[]{:S(2)}) async-start(), calls=%async_computation.4 | async-start | bytes 2097152 | tf_op jit(solution)/shard_map/psum | solution.py:49
  9.2 3.5 copy-start.23
  10.0 4.9 copy-start.25
  10.0 4.9 copy-start.27
  10.0 4.9 copy-start.29
  10.0 2.7 copy-start.2
  10.0 2.7 copy-start.22
  14.8 1.4 copy-start.11
  14.9 2.7 copy-start.3
  17.6 87.1 %all-reduce.12.cloned.1.call-start = ((), (), s32[]{:S(2)}) async-start(), calls=%async_computation.5 | async-start | bytes 2097152 | tf_op jit(solution)/shard_map/psum | solution.py:66
  29.6 29.3 %copy-start.21 = (f32[1024]{0:T(1024)S(1)}, f32[1024]{0:T(1024)}, u32[]{:S(2)}) copy-start(f32[1024]{0:T(1024)} %param.14) | copy-start | bytes 12292
  58.9 4.0 copy-start.13
  58.9 6.4 %slice-start = ((s8[4718592]{0:T(1024)(128)(4,1)}), s8[4194304]{0:T(1024)(128)(4,1)S(1)}, s32[]{:S(2)}) async-start(s8[4718592]{0:T(1024)(128)(4,1)} %bitcast.114), calls=%async_computation.11 | async-start | bytes 8388608
  62.9 1.4 copy-start.5
  62.9 2.4 slice-start.1
  67.8 96.7 %all-reduce.14.cloned.1.call-start = ((), (), s32[]{:S(2)}) async-start(), calls=%async_computation.10 | async-start | bytes 4194304 | tf_op jit(solution)/shard_map/psum | solution.py:57
  104.7 1.6 copy-start.10
  104.7 1.7 copy-start.14
  104.7 1.7 copy-start.34
  106.3 1.2 copy-start.9
  106.3 1.4 copy-start.12
  107.7 1.4 copy-start.26
  107.7 1.4 copy-start.28
  107.7 1.4 copy-start.30
  109.1 1.6 copy-start.7
  112.4 218.2 %reduce-scatter.9.cloned.1.call-start = ((), (), s32[]{:S(2)}) async-start(), calls=%async_computation.8 | async-start | bytes 10616832 | tf_op jit(solution)/shard_map/reduce_scatter | solution.py:105
  124.2 2.7 copy-start.24
  124.2 274.1 %reduce-scatter.7.cloned.1.call-start = ((), (), s32[]{:S(2)}) async-start(), calls=%async_computation.7 | async-start | bytes 1179648 | tf_op jit(solution)/shard_map/reduce_scatter | solution.py:104
  126.8 349.4 %reduce-scatter.5.cloned.1.call-start = ((), (), s32[]{:S(2)}) async-start(), calls=%async_computation.6 | async-start | bytes 3538944 | tf_op jit(solution)/shard_map/reduce_scatter | solution.py:103
  130.5 445.3 %reduce-scatter.11.cloned.1.call-start = ((), (), s32[]{:S(2)}) async-start(), calls=%async_computation.9 | async-start | bytes 5308416 | tf_op jit(solution)/shard_map/reduce_scatter | solution.py:106
  134.8 70.5 %copy-start.35 = (f32[256]{0:T(256)S(1)}, f32[256]{0:T(256)}, u32[]{:S(2)}) copy-start(f32[256]{0:T(256)} %get-tuple-element.51) | copy-start | bytes 3076
  (13 other events, 11.1 us)
Sparse Core Ops, SparseCore 0:
  17.7 39.0 all-reduce.9
  67.9 36.7 all-reduce.11
  112.5 51.8 all-reduce.13
  167.9 162.6 reduce-scatter.8
  334.4 63.8 reduce-scatter.6
  402.3 73.8 reduce-scatter.4
  480.4 95.2 reduce-scatter.10
where the time goes:
time: 583 us
  waiting for transfers between devices  452 us (78%)
  blocking collectives  39.2 us (7%)
  matrix products  32.6 us (6%)
  local copies, waits for them, and re-layouts  26.8 us (5%)
  other arithmetic  16.9 us (3%)
  between operations  14.5 us (2%)
    reduce_scatter x1, waiting for transfers between devices, body(): lax.psum_scatter(grad_gu, 'dp', scatter_dimension=0, tiled=True)  122 us
    reduce_scatter x1, waiting for transfers between devices, body(): lax.psum_scatter(grad_down, 'dp', scatter_dimension=1, tiled=True)  99.5 us
    reduce_scatter x1, waiting for transfers between devices, body(): lax.psum_scatter(grad_in, 'dp', scatter_dimension=0, tiled=True)  77.9 us
    reduce_scatter x1, waiting for transfers between devices, body(): lax.psum_scatter(grad_out, 'dp', scatter_dimension=1, tiled=True)  64.5 us
    psum x1, blocking collectives, body(): sum_taps, sum_n1, sum_n2 = lax.psum((gtaps, gn1, gn2), 'dp')  39.2 us
    psum x1, waiting for transfers between devices, body(): d_normed2 = lax.psum(by_transpose(d_gu, w_gu_flat), 'tensor')  32.2 us
    psum x1, waiting for transfers between devices, body(): lax.psum(jnp.dot(hidden, w_down, preferred_element_type=jnp.float32), 'te...  28.9 us
    psum x1, waiting for transfers between devices, body(): lax.psum(jnp.dot(gated, w_out, preferred_element_type=jnp.float32), 'tens...  27.1 us
  transfers between devices with their start and end apart: 7, of which 7 were waited for; matrix products, arithmetic and copies ran while one was open for 8% of the time, Pallas kernels for 0%

commit v1 on v0

--- a/solution.py
+++ b/solution.py
@@ -63,7 +63,7 @@
     d_up = d_hidden * act * sig
     d_gu = jnp.stack([d_act, d_up], axis=1).astype(jnp.bfloat16).reshape(rows, 2 * hid)
     grad_gu = cross(normed2, d_gu).reshape(width, 2, hid)
-    d_normed2 = lax.psum(by_transpose(d_gu, w_gu_flat), "tensor")
+    d_normed2 = jnp.sum(lax.all_gather(by_transpose(d_gu, w_gu_flat), "tensor"), axis=0)
     gn2 = jnp.sum(d_normed2 * resid * s2, axis=0)
     weighted2 = d_normed2 * norm_second
     d_resid = (

time: 583 us -> 584 us (level)
    psum x1 -> x0, waiting for transfers between devices: 32.2 us -> none  [body(): d_normed2 = lax.psum(by_transpose(d_gu, w_gu_flat), 'tensor')]
    all_gather x0 -> x1, waiting for transfers between devices: none -> 30.4 us  [body(): lax.all_gather(by_transpose(d_gu, w_gu_flat), 'tensor')]
    unnamed x79 -> x87, local copies, waits for them, and re-layouts: 16.7 us -> 18.4 us
  transfers between devices with their start and end apart: 7 -> 7, of which waited for: 7 -> 7; matrix products, arithmetic and copies ran while one was open for 8% -> 7% of each run, Pallas kernels for 0% -> 0%
where the time goes in v1:
time: 584 us; the launch traced here: 583 us
  waiting for transfers between devices  455 us (78%)
  blocking collectives  39.2 us (7%)
  matrix products  28.6 us (5%)
  local copies, waits for them, and re-layouts  27.5 us (5%)
  other arithmetic  17.3 us (3%)
  between operations  14.5 us (2%)
    reduce_scatter x1, waiting for transfers between devices, body(): lax.psum_scatter(grad_gu, 'dp', scatter_dimension=0, tiled=True)  122 us
    reduce_scatter x1, waiting for transfers between devices, body(): lax.psum_scatter(grad_down, 'dp', scatter_dimension=1, tiled=True)  99.2 us
    reduce_scatter x1, waiting for transfers between devices, body(): lax.psum_scatter(grad_in, 'dp', scatter_dimension=0, tiled=True)  78.7 us
    reduce_scatter x1, waiting for transfers between devices, body(): lax.psum_scatter(grad_out, 'dp', scatter_dimension=1, tiled=True)  64.5 us
    psum x1, blocking collectives, body(): sum_taps, sum_n1, sum_n2 = lax.psum((gtaps, gn1, gn2), 'dp')  39.2 us
    psum x1, waiting for transfers between devices, body(): lax.psum(jnp.dot(hidden, w_down, preferred_element_type=jnp.float32), 'te...  33.3 us
    all_gather x1, waiting for transfers between devices, body(): lax.all_gather(by_transpose(d_gu, w_gu_flat), 'tensor')  30.4 us
    psum x1, waiting for transfers between devices, body(): lax.psum(jnp.dot(gated, w_out, preferred_element_type=jnp.float32), 'tens...  27.1 us
  transfers between devices with their start and end apart: 7, of which 7 were waited for; matrix products, arithmetic and copies ran while one was open for 7% of the time, Pallas kernels for 0%

profile of v1, /device:TPU:0, one launch (start us, length us, event | category | flops | bytes accessed | tf_op | source)
XLA Modules:
  0.0 582.8 jit_solution(18272814526753728526)
XLA Ops:
  7.2 1.4 fusion.9
  10.1 2.7 copy.24
  12.7 2.1 fusion.2
  16.3 1.3 fusion.34
  17.7 5.4 copy.37
  23.0 6.7 %copy.25 = bf16[2304,1024]{1,0:T(8,128)(2,1)} copy(bf16[2304,1024]{0,1:T(8,128)(2,1)} %bitcast.108) | data formatting | bytes 9437184 | tf_op jit(solution)/shard_map/dot_general | solution.py:53
  29.7 27.1 %all-reduce.9.cloned.1.call-done = f32[256,1024]{1,0:T(8,128)} async-done(((f32[256,1024]{1,0:T(8,128)}), f32[256,1024]{1,0:T(8,128)}) %all-reduce.9.cloned.1.call-update) | async-done | bytes 1048592 | tf_op jit(solution)/shard_map/psum | solution.py:49
  56.8 1.6 multiply_reduce_fusion.2
  58.9 3.9 fusion.30
  62.9 1.2 multiply_bitcast_fusion.1
  65.4 2.4 fusion.4
  67.9 2.0 multiply_convert_fusion
  70.6 1.9 fusion.35
  72.5 30.4 %all-gather.3.cloned.1.call-done = f32[1024,1024]{1,0:T(8,128)} async-done(((f32[256,1024]{1,0:T(8,128)}), f32[1024,1024]{1,0:T(8,128)}) %all-gather.3.cloned.1.call-update) | async-done | bytes 4194320 | tf_op jit(solution)/shard_map/all_gather | solution.py:66
  102.9 2.7 reduce_sum.92
  108.0 1.1 multiply_reduce_fusion.5
  111.0 1.6 convolution_bitcast_fusion
  112.9 1.4 maximum_convert_fusion
  114.3 1.4 copy.29
  115.7 6.5 %fusion.7 = f32[1024,2,1152]{2,0,1:T(8,128)} fusion(bf16[256,2,1152]{0,2,1:T(8,128)(2,1)} %copy.29, f32[256,1024]{1,0:T(8,128)S(1)} %get-tuple-element.43, f32[1024]{0:T(1024)S(1)} %copy-done.25, f32[256]{0:T(256)S(1)} %get-tuple-element.54), kind=kOutput, calls=%fused_computation.15 | convolution fusion | flops 1208745984 | bytes 11670528 | tf_op jit(solution)/shard_map/dot_general | solution.py:20
  122.3 1.3 fusion.23
  123.7 3.0 fusion.36
  127.8 2.3 fusion.19
  130.9 33.3 %all-reduce.11.cloned.1.call-done = (f32[256,1024]{1,0:T(8,128)}, f32[256,1024]{1,0:T(8,128)}) async-done(((f32[256,1024]{1,0:T(8,128)}, f32[256,1024]{1,0:T(8,128)}), (f32[256,1024]{1,0:T(8,128)}, f32[256,1024]{1,0:T(8,128)})) %all-reduce.11.cloned.1.call-update) | async-done | bytes 2097168 | tf_op jit(solution)/shard_map/psum | solution.py:57
  164.2 1.5 fusion.16
  165.7 39.2 %all-reduce.4 = (f32[1024]{0:T(1024)}, f32[3,256]{1,0:T(4,128)}, f32[1024]{0:T(1024)}) all-reduce(f32[1024]{0:T(1024)S(1)} %get-tuple-element.29, f32[3,256]{1,0:T(4,128)S(1)} %pad_maximum_fusion, f32[1024]{0:T(1024)S(1)} %get-tuple-element.27), channel_id=1, replica_groups=mesh['dp'=8,'tensor'=4] {'dp'}, use_global_device_ids=true, to_apply=%region_9.0 | all-reduce | flops 2816 | bytes 22528 | tf_op jit(solution)/shard_map/psum | solution.py:108
  205.0 3.6 fusion.13
  208.6 121.7 %reduce-scatter.9.cloned.1.call-done = f32[128,2,1152]{2,0,1:T(8,128)} async-done(((f32[1024,2,1152]{2,0,1:T(8,128)}), f32[128,2,1152]{2,0,1:T(8,128)}) %reduce-scatter.9.cloned.1.call-update) | async-done | bytes 1179664 | tf_op jit(solution)/shard_map/reduce_scatter | solution.py:105
  330.3 3.2 copy.31
  333.5 64.5 %reduce-scatter.7.cloned.1.call-done = f32[256,128]{1,0:T(8,128)} async-done(((f32[256,1024]{1,0:T(8,128)}), f32[256,128]{1,0:T(8,128)}) %reduce-scatter.7.cloned.1.call-update) | async-done | bytes 131088 | tf_op jit(solution)/shard_map/reduce_scatter | solution.py:104
  398.0 99.2 %reduce-scatter.11.cloned.1.call-done = f32[1152,128]{1,0:T(8,128)} async-done(((f32[1152,1024]{1,0:T(8,128)}), f32[1152,128]{1,0:T(8,128)}) %reduce-scatter.11.cloned.1.call-update) | async-done | bytes 589840 | tf_op jit(solution)/shard_map/reduce_scatter | solution.py:106
  497.2 78.7 %reduce-scatter.5.cloned.1.call-done = f32[128,3,256]{2,0,1:T(8,128)} async-done(((f32[1024,3,256]{2,0,1:T(8,128)}), f32[128,3,256]{2,0,1:T(8,128)}) %reduce-scatter.5.cloned.1.call-update) | async-done | bytes 393232 | tf_op jit(solution)/shard_map/reduce_scatter | solution.py:103
  (114 shorter events, 11.9 us)
Async XLA Ops:
  7.2 55.7 %copy-start = (bf16[1152,1024]{1,0:T(8,128)(2,1)S(1)}, bf16[1152,1024]{1,0:T(8,128)(2,1)}, u32[]{:S(2)}) copy-start(bf16[1152,1024]{1,0:T(8,128)(2,1)} %param.16) | copy-start | bytes 7077892
  7.2 49.6 %all-reduce.9.cloned.1.call-start = ((), (), s32[]{:S(2)}) async-start(), calls=%async_computation.4 | async-start | bytes 2097152 | tf_op jit(solution)/shard_map/psum | solution.py:49
  9.2 3.5 copy-start.27
  10.0 4.9 copy-start.29
  10.0 4.9 copy-start.31
  10.0 4.9 copy-start.33
  10.0 2.7 copy-start.3
  10.0 2.7 copy-start.26
  14.9 1.4 copy-start.13
  14.9 2.7 copy-start.5
  17.6 85.3 %all-gather.3.cloned.1.call-start = ((), (), s32[]{:S(2)}) async-start(), calls=%async_computation.9 | async-start | bytes 5242880 | tf_op jit(solution)/shard_map/all_gather | solution.py:66
  29.7 29.2 %copy-start.25 = (f32[1024]{0:T(1024)S(1)}, f32[1024]{0:T(1024)}, u32[]{:S(2)}) copy-start(f32[1024]{0:T(1024)} %param.14) | copy-start | bytes 12292
  58.9 4.0 copy-start.15
  58.9 6.4 %slice-start = ((s8[4718592]{0:T(1024)(128)(4,1)}), s8[4194304]{0:T(1024)(128)(4,1)S(1)}, s32[]{:S(2)}) async-start(s8[4718592]{0:T(1024)(128)(4,1)} %bitcast.115), calls=%async_computation.11 | async-start | bytes 8388608
  62.9 1.5 copy-start.7
  62.9 2.5 slice-start.1
  67.8 96.4 %all-reduce.11.cloned.1.call-start = ((), (), s32[]{:S(2)}) async-start(), calls=%async_computation.10 | async-start | bytes 4194304 | tf_op jit(solution)/shard_map/psum | solution.py:57
  108.0 14.3 %copy-start.2 = (f32[256,1024]{1,0:T(8,128)}, f32[256,1024]{1,0:T(8,128)S(1)}, u32[]{:S(2)}) copy-start(f32[256,1024]{1,0:T(8,128)S(1)} %multiply_subtract_fusion) | copy-start | bytes 3145732
  108.0 1.4 copy-start.30
  108.0 1.4 copy-start.32
  108.0 1.4 copy-start.34
  109.4 1.5 copy-start.10
  109.7 2.9 copy-start.18
  110.4 2.2 copy-start.20
  112.7 217.7 %reduce-scatter.9.cloned.1.call-start = ((), (), s32[]{:S(2)}) async-start(), calls=%async_computation.7 | async-start | bytes 10616832 | tf_op jit(solution)/shard_map/reduce_scatter | solution.py:105
  122.2 1.5 copy-start.9
  122.2 1.5 copy-start.17
  122.2 275.8 %reduce-scatter.7.cloned.1.call-start = ((), (), s32[]{:S(2)}) async-start(), calls=%async_computation.6 | async-start | bytes 1179648 | tf_op jit(solution)/shard_map/reduce_scatter | solution.py:104
  123.6 373.6 %reduce-scatter.11.cloned.1.call-start = ((), (), s32[]{:S(2)}) async-start(), calls=%async_computation.8 | async-start | bytes 5308416 | tf_op jit(solution)/shard_map/reduce_scatter | solution.py:106
  126.7 449.2 %reduce-scatter.5.cloned.1.call-start = ((), (), s32[]{:S(2)}) async-start(), calls=%async_computation.5 | async-start | bytes 3538944 | tf_op jit(solution)/shard_map/reduce_scatter | solution.py:103
  130.2 74.8 %copy-start.39 = (f32[256]{0:T(256)S(1)}, f32[256]{0:T(256)}, u32[]{:S(2)}) copy-start(f32[256]{0:T(256)} %get-tuple-element.51) | copy-start | bytes 3076
  205.0 370.9 %copy-start.1 = (bf16[1152,1024]{1,0:T(8,128)(2,1)S(1)}, bf16[1152,1024]{1,0:T(8,128)(2,1)}, u32[]{:S(2)}) copy-start(bf16[1152,1024]{1,0:T(8,128)(2,1)} %param.16) | copy-start | bytes 7077892
  (17 other events, 16.7 us)
Sparse Core Ops, SparseCore 0:
  17.7 39.0 all-reduce.8
  67.9 34.9 all-gather.2
  112.8 51.3 all-reduce.10
  167.6 162.6 reduce-scatter.8
  334.1 63.8 reduce-scatter.6
  402.1 95.0 reduce-scatter.10
  501.4 74.4 reduce-scatter.4
